TPU v7x, 128 devices: a whole 4x4x4 slice. The times are simulated.
128 devices in a mesh: seq: 32 (over z, x, core), exp: 4 (over y).
Axes of the slice: x: 4, y: 4, z: 4, core: 2. Of those that a mesh axis runs over, the one named last changes fastest.
Arguments:
- queries: bfloat16 [4096, 5120], P('seq', 'exp'), may hold values from -48 to 48
- keys_values: bfloat16 [2, 4096, 1024], P(None, 'seq', 'exp'), may hold values from -8 to 8
- residual: bfloat16 [4096, 5120], P(('seq', 'exp')), may hold values from -6 to 6
- norm_gain: float32 [5120], replicated, may hold values from 0.1 to 1.9
- route_logit: float32 [4096], P(('seq', 'exp')), may hold values from -2 to -1
- expert_ids: int32 [4096, 1], P(('seq', 'exp')), may hold values from 0 to 3; in each aligned block of 32 rows (0 to 31, 32 to 63, ...) at most 12 rows name the same one
- out_weight: bfloat16 [5120, 5120], P('exp'), may hold values from -0.078125 to 0.078125
- gate_weight: bfloat16 [4, 5120, 8192], P('exp', None, 'seq'), may hold values from -0.25 to 0.25
- up_weight: bfloat16 [4, 5120, 8192], P('exp', None, 'seq'), may hold values from -0.25 to 0.25
- down_weight: bfloat16 [4, 8192, 5120], P('exp', 'seq'), may hold values from -0.125 to 0.125
Outputs:
- layer_output: bfloat16 [4096, 5120], P(('seq', 'exp'))
Inputs may be any that keep to these rules, and one draw needn't show every extreme that they name: `expert_ids`: in each aligned block of 32 tokens (the tokens of one device) no expert is named more than 12 times, a bound that some block reaches.
All inputs are finite; a program needn't handle non-finite values.
Results may differ from a plain program's by a relative error of at most 0.015.
Values may be sent and summed in bfloat16 or wider, within the bound.
No kernel may reach another device: no remote copies, remote signals or barrier semaphores. Data moves between devices by JAX's collectives and lax.ppermute only.
A program may use at most 128 MiB of HBM per device.

v0:
```python
import jax
import jax.numpy as jnp
from jax import lax
from jax.sharding import PartitionSpec as P

D = 5120
HD = 128


def in_blocks(shard, dim, devices):
    dims = shard.shape
    parts = shard.reshape(*dims[:dim], devices, dims[dim] // devices, *dims[dim + 1 :])
    return jnp.moveaxis(parts, dim, 0)


def sent_and_summed(shard, axis, dim):
    devices = lax.axis_size(axis)
    parts = lax.all_to_all(in_blocks(shard, dim, devices), axis, 0, 0, tiled=True)
    return jnp.sum(parts.astype(jnp.float32), axis=0)


def body(
    queries,
    keys_values,
    residual,
    norm_gain,
    route_logit,
    expert_ids,
    out_weight,
    gate_weight,
    up_weight,
    down_weight,
):
    seq_rows = queries.shape[0]
    heads_here = queries.shape[1] // HD
    kv_here = keys_values.shape[2] // HD
    group = heads_here // kv_here
    seq_index = lax.axis_index("seq")
    span_devs = lax.axis_size("seq")
    my_position = seq_index * seq_rows + jnp.arange(seq_rows, dtype=jnp.int32)
    my_span = seq_index // span_devs
    scale = 1.0 / HD**0.5
    query_heads = queries.reshape(seq_rows, kv_here, group, HD)
    piece = lax.all_gather(keys_values, "seq", axis=1, tiled=True)
    peak = jnp.full((kv_here, group, seq_rows), -1e30, jnp.float32)
    count = piece.shape[1]
    key_position = jnp.arange(count, dtype=jnp.int32)
    same_span = key_position // (span_devs * seq_rows) == my_span
    allowed = same_span[None, :] & (key_position[None, :] <= my_position[:, None])
    key_rows = piece[0].reshape(count, kv_here, HD)
    value_rows = piece[1].reshape(count, kv_here, HD)
    score = (
        jnp.einsum("skgd,nkd->kgsn", query_heads, key_rows, preferred_element_type=jnp.float32)
        * scale
    )
    score = jnp.where(allowed, score, -1e30)
    fresh = jnp.maximum(peak, jnp.max(score, axis=-1))
    expo = jnp.where(allowed, jnp.exp(score - fresh[..., None]), 0.0)
    total = jnp.sum(expo, axis=-1)
    accum = jnp.einsum(
        "kgsn,nkd->kgsd", expo.astype(jnp.bfloat16), value_rows, preferred_element_type=jnp.float32
    )
    state = (fresh, total, accum)
    peak, total, accum = state
    attended = (
        jnp.transpose(accum / total[..., None], (2, 0, 1, 3))
        .reshape(seq_rows, heads_here * HD)
        .astype(jnp.bfloat16)
    )
    rows = attended
    projected = sent_and_summed(
        jnp.dot(rows, out_weight, preferred_element_type=jnp.float32).astype(jnp.bfloat16), "exp", 0
    )
    stream = residual.astype(jnp.float32) + projected
    mixed = stream.astype(jnp.bfloat16)
    stream = mixed.astype(jnp.float32)
    mean_square = jnp.mean(stream * stream, axis=-1, keepdims=True)
    routed_in = (
        stream * lax.rsqrt(mean_square + 1e-05) * norm_gain * jax.nn.sigmoid(route_logit)[:, None]
    ).astype(jnp.bfloat16)
    token_rows = residual.shape[0]
    capacity = 3 * token_rows // 8
    experts = lax.axis_size("exp")
    ids = expert_ids[:, 0]
    onehot = (ids[:, None] == jnp.arange(experts, dtype=jnp.int32)[None, :]).astype(jnp.int32)
    rank = jnp.sum((jnp.cumsum(onehot, axis=0) - onehot) * onehot, axis=1)
    slot = ids * capacity + rank
    placing = (jnp.arange(experts * capacity, dtype=jnp.int32)[:, None] == slot[None, :]).astype(
        jnp.bfloat16
    )
    outgoing = (
        jnp.dot(placing, routed_in, preferred_element_type=jnp.float32)
        .astype(jnp.bfloat16)
        .reshape(experts, capacity, D)
    )
    arrived = lax.all_to_all(outgoing, "exp", split_axis=0, concat_axis=0, tiled=True).reshape(
        experts * capacity, D
    )
    piece = lax.all_gather(arrived, "seq", axis=0, tiled=True)
    gate = jnp.dot(piece, gate_weight[0], preferred_element_type=jnp.float32)
    up = jnp.dot(piece, up_weight[0], preferred_element_type=jnp.float32)
    hidden = (jax.nn.silu(gate) * up).astype(jnp.bfloat16)
    rows = hidden
    summed = lax.psum_scatter(
        jnp.dot(rows, down_weight[0], preferred_element_type=jnp.float32).astype(jnp.bfloat16),
        "seq",
        scatter_dimension=0,
        tiled=True,
    )
    returned = lax.all_to_all(
        summed.reshape(experts, capacity, D), "exp", split_axis=0, concat_axis=0, tiled=True
    )
    back_rows = returned.reshape(experts * capacity, D)
    picking = (slot[:, None] == jnp.arange(experts * capacity, dtype=jnp.int32)[None, :]).astype(
        jnp.bfloat16
    )
    routed = jnp.dot(picking, back_rows, preferred_element_type=jnp.float32)
    return (stream + routed).astype(jnp.bfloat16)


def solution(mesh):
    in_specs = (
        P("seq", "exp"),
        P(None, "seq", "exp"),
        P(("seq", "exp"), None),
        P(),
        P(("seq", "exp")),
        P(("seq", "exp"), None),
        P("exp", None),
        P("exp", None, "seq"),
        P("exp", None, "seq"),
        P("exp", "seq", None),
    )
    out_specs = P(("seq", "exp"), None)
    return jax.shard_map(body, mesh=mesh, in_specs=in_specs, out_specs=out_specs, check_vma=False)
```

profile of v0, /device:TPU:0, one launch (start us, length us, event | category | flops | bytes accessed | tf_op | source)
XLA Modules:
  0.0 383.5 jit_solution(18373603022265235883)
XLA Ops:
  6.5 1.8 copy.14
  8.4 1.9 copy.15
  10.3 2.1 fusion.14
  12.4 48.3 %all-gather.3.cloned.1.call-done = bf16[2,4096,256]{1,2,0:T(8,128)(2,1)} async-done(((bf16[2,128,256]{1,2,0:T(8,128)(2,1)}), bf16[2,4096,256]{1,2,0:T(8,128)(2,1)}) %all-gather.3.cloned.1.call-update) | async-done | bytes 4194320 | tf_op jit(solution)/shard_map/all_gather | solution.py:44
  60.8 4.7 %fusion.47 = (bf16[1,4096,256]{1,2,0:T(8,128)(2,1)}, bf16[1,4096,256]{1,2,0:T(8,128)(2,1)}) fusion(bf16[2,4096,256]{1,2,0:T(8,128)(2,1)} %all-gather.3.cloned.1.call-done), kind=kLoop, calls=%fused_computation.61 | loop fusion | bytes 8388608 | tf_op jit(solution)/shard_map/slice | solution.py:50
  65.5 5.0 %fusion = (f32[2,5,128]{2,1,0:T(8,128)S(1)}, f32[2,4096,128,5]{2,1,3,0:T(8,128)S(1)}) fusion(pred[128,4096]{0,1:T(8,128)(4,1)S(1)} %fusion.14, bf16[4096,2,128,1]{0,2,3,1:T(8,128)(2,1)} %bitcast.66, bf16[128,2,5,128]{0,3,2,1:T(8,128)(2,1)} %bitcast.69), kind=kOutput, calls=%fused_computation.3 | convolution fusion | flops 1357904640 | bytes 23925760 | tf_op jit(solution)/shard_map/skgd,nkd->kgsn/dot_general | solution.py:53
  70.5 5.1 %fusion.1 = f32[2,5,128]{2,1,0:T(8,128)S(1)} fusion(f32[2,4096,128,5]{2,1,3,0:T(8,128)S(1)} %get-tuple-element.10, f32[2,5,128]{2,1,0:T(8,128)S(1)} %broadcast_maximum_fusion, pred[128,4096]{0,1:T(8,128)(4,1)S(1)} %fusion.14), kind=kLoop, calls=%fused_computation.4 | loop fusion | flops 26213120 | bytes 21506048 | tf_op jit(solution)/shard_map/reduce_sum | solution.py:59
  75.6 1.9 copy-done.1
  77.5 13.1 %fusion.21 = bf16[128,2,5,128]{0,3,2,1:T(8,128)(2,1)S(1)} fusion(bf16[4096,2,128,1]{0,2,3,1:T(8,128)(2,1)} %bitcast.68, f32[2,4096,128,5]{2,1,3,0:T(8,128)} %copy-done.1, f32[2,5,128]{2,1,0:T(8,128)S(1)} %broadcast_maximum_fusion, pred[128,4096]{0,1:T(8,128)(4,1)S(1)} %fusion.14, f32[128,2,5]{0,2,1:T(8,128)S(1)} %bitcast.71), kind=kOutput, calls=%fused_computation.23 | convolution fusion | flops 1368719360 | bytes 23930880 | tf_op jit(solution)/shard_map/kgsn,nkd->kgsd/dot_general | solution.py:60
  90.6 7.8 %convolution_convert_fusion.1 = bf16[128,5120]{1,0:T(8,128)(2,1)} fusion(bf16[128,1280]{0,1:T(8,128)(2,1)S(1)} %bitcast.70, bf16[1280,5120]{1,0:T(8,128)(2,1)} %param.16), kind=kOutput, calls=%fused_computation.8 | convolution fusion | flops 1678376960 | bytes 14745600 | tf_op jit(solution)/shard_map/dot_general | solution.py:72
  98.4 4.4 %all-to-all-start = ((bf16[4,32,5120]{2,1,0:T(8,128)(2,1)}), bf16[4,32,5120]{2,1,0:T(8,128)(2,1)}, u32[]{:S(2)}, u32[]{:S(2)}) async-start(bf16[4,32,5120]{2,1,0:T(8,128)(2,1)} %bitcast.67), calls=%async_computation | async-start | bytes 2621440 | tf_op jit(solution)/shard_map/all_to_all | solution.py:18
  102.8 0.2 all-gather.5.cloned.1.call-start
  103.0 0.1 fusion.38
  103.1 0.1 reduce_window_sum.11
  103.1 0.2 select_reduce_fusion
  103.3 18.1 %all-to-all-done = bf16[4,32,5120]{2,1,0:T(8,128)(2,1)} async-done(((bf16[4,32,5120]{2,1,0:T(8,128)(2,1)}), bf16[4,32,5120]{2,1,0:T(8,128)(2,1)}, u32[]{:S(2)}, u32[]{:S(2)}) %all-to-all-start) | async-done | bytes 1310752 | tf_op jit(solution)/shard_map/all_to_all | solution.py:18
  121.4 1.6 convert_reduce_fusion
  123.0 0.2 fusion.27
  123.3 0.7 copy-done.2
  124.0 1.1 convolution_convert_fusion.2
  125.1 1.1 reshape.63
  126.3 13.8 %all_to_all.15 = bf16[4,12,5120]{2,1,0:T(8,128)(2,1)} all-to-all(bf16[4,12,5120]{2,1,0:T(8,128)(2,1)S(1)} %reshape.63), channel_id=1, replica_groups=mesh['seq'=32,'exp'=4] {'exp'}, dimensions={0} | all-to-all | bytes 983040 | tf_op jit(solution)/shard_map/all_to_all | solution.py:96
  140.0 2.0 reshape.64
  142.1 68.0 %all-gather.5.cloned.1.call-done = bf16[1536,5120]{1,0:T(8,128)(2,1)} async-done(((bf16[48,5120]{1,0:T(8,128)(2,1)}), bf16[1536,5120]{1,0:T(8,128)(2,1)}) %all-gather.5.cloned.1.call-update) | async-done | bytes 15728656 | tf_op jit(solution)/shard_map/all_gather | solution.py:99
  210.1 11.7 %fusion.9 = f32[1536,256]{1,0:T(8,128)} fusion(bf16[1536,5120]{1,0:T(8,128)(2,1)} %all-gather.5.cloned.1.call-done, bf16[1,5120,256]{2,1,0:T(8,128)(2,1)} %param.17), kind=kOutput, calls=%fused_computation.15 | convolution fusion | flops 4026531840 | bytes 19922944 | tf_op jit(solution)/shard_map/dot_general | solution.py:100
  221.8 23.8 %convolution_convert_fusion = bf16[1536,5120]{1,0:T(8,128)(2,1)} fusion(bf16[1,256,5120]{2,1,0:T(8,128)(2,1)S(1)} %copy-done, bf16[1536,5120]{1,0:T(8,128)(2,1)} %all-gather.5.cloned.1.call-done, bf16[1,5120,256]{2,1,0:T(8,128)(2,1)} %param.18, f32[1536,256]{1,0:T(8,128)} %fusion.9), kind=kOutput, calls=%fused_computation.2 | convolution fusion | flops 8063287296 | bytes 38273024 | tf_op jit(solution)/shard_map/dot_general | solution.py:105
  245.6 112.5 %reduce-scatter.2.cloned.1.call-done = bf16[48,5120]{1,0:T(8,128)(2,1)} async-done(((bf16[1536,5120]{1,0:T(8,128)(2,1)}), bf16[48,5120]{1,0:T(8,128)(2,1)}) %reduce-scatter.2.cloned.1.call-update) | async-done | bytes 491536 | tf_op jit(solution)/shard_map/reduce_scatter | solution.py:104
  358.1 2.0 reshape.65
  360.1 4.3 %all-to-all-start.2 = ((bf16[4,12,5120]{2,1,0:T(8,128)(2,1)}), bf16[4,12,5120]{2,1,0:T(8,128)(2,1)S(1)}, u32[]{:S(2)}, u32[]{:S(2)}) async-start(bf16[4,12,5120]{2,1,0:T(8,128)(2,1)} %reshape.65), calls=%async_computation.3 | async-start | bytes 1310720 | tf_op jit(solution)/shard_map/all_to_all | solution.py:110
  364.4 9.6 %all-to-all-done.2 = bf16[4,12,5120]{2,1,0:T(8,128)(2,1)S(1)} async-done(((bf16[4,12,5120]{2,1,0:T(8,128)(2,1)}), bf16[4,12,5120]{2,1,0:T(8,128)(2,1)S(1)}, u32[]{:S(2)}, u32[]{:S(2)}) %all-to-all-start.2) | async-done | bytes 491552 | tf_op jit(solution)/shard_map/all_to_all | solution.py:110
  374.0 0.9 reshape.66
  374.9 2.1 fusion.6
  (23 shorter events, 0.2 us)
Async XLA Ops:
  6.5 215.3 %copy-start = (bf16[1,256,5120]{2,1,0:T(8,128)(2,1)S(1)}, bf16[1,256,5120]{2,1,0:T(8,128)(2,1)}, u32[]{:S(2)}) copy-start(bf16[1,256,5120]{2,1,0:T(8,128)(2,1)} %param.19) | copy-start | bytes 7864324
  6.5 54.2 %all-gather.3.cloned.1.call-start = ((), (), s32[]{:S(2)}) async-start(), calls=%async_computation.4 | async-start | bytes 4325376 | tf_op jit(solution)/shard_map/all_gather | solution.py:44
  70.5 7.0 %copy-start.1 = (f32[2,4096,128,5]{2,1,3,0:T(8,128)}, f32[2,4096,128,5]{2,1,3,0:T(8,128)S(1)}, u32[]{:S(2)}) copy-start(f32[2,4096,128,5]{2,1,3,0:T(8,128)S(1)} %get-tuple-element.10) | copy-start | bytes 62914564
  90.5 12.5 %copy-start.4 = (s32[32,1]{0,1:T(1,128)S(1)}, s32[32,1]{0,1:T(1,128)}, u32[]{:S(2)}) copy-start(s32[32,1]{0,1:T(1,128)} %param.15) | copy-start | bytes 388
  90.6 32.5 %copy-start.3 = (bf16[32,5120]{1,0:T(8,128)(2,1)S(1)}, bf16[32,5120]{1,0:T(8,128)(2,1)}, u32[]{:S(2)}) copy-start(bf16[32,5120]{1,0:T(8,128)(2,1)} %param.12) | copy-start | bytes 983044
  98.3 24.9 %copy-start.5 = (f32[32]{0:T(128)S(1)}, f32[32]{0:T(128)}, u32[]{:S(2)}) copy-start(f32[32]{0:T(128)} %param.14) | copy-start | bytes 388
  98.3 25.6 %copy-start.6 = (f32[5120]{0:T(1024)S(1)}, f32[5120]{0:T(1024)}, u32[]{:S(2)}) copy-start(f32[5120]{0:T(1024)} %param.13) | copy-start | bytes 61444
  98.4 23.1 %all-to-all-start = ((bf16[4,32,5120]{2,1,0:T(8,128)(2,1)}), bf16[4,32,5120]{2,1,0:T(8,128)(2,1)}, u32[]{:S(2)}, u32[]{:S(2)}) async-start(bf16[4,32,5120]{2,1,0:T(8,128)(2,1)} %bitcast.67), calls=%async_computation | async-start | bytes 2621440 | tf_op jit(solution)/shard_map/all_to_all | solution.py:18
  102.8 107.3 %all-gather.5.cloned.1.call-start = ((), (), s32[]{:S(2)}) async-start(), calls=%async_computation.5 | async-start | bytes 16220160 | tf_op jit(solution)/shard_map/all_gather | solution.py:99
  123.3 0.7 copy-start.2
  142.0 216.1 %reduce-scatter.2.cloned.1.call-start = ((), (), s32[]{:S(2)}) async-start(), calls=%async_computation.6 | async-start | bytes 16220160 | tf_op jit(solution)/shard_map/reduce_scatter | solution.py:104
  360.1 13.9 %all-to-all-start.2 = ((bf16[4,12,5120]{2,1,0:T(8,128)(2,1)}), bf16[4,12,5120]{2,1,0:T(8,128)(2,1)S(1)}, u32[]{:S(2)}, u32[]{:S(2)}) async-start(bf16[4,12,5120]{2,1,0:T(8,128)(2,1)} %reshape.65), calls=%async_computation.3 | async-start | bytes 1310720 | tf_op jit(solution)/shard_map/all_to_all | solution.py:110
Sparse Core Ops, SparseCore 0:
  9.5 51.1 all-gather.2
  142.2 67.8 all-gather.4
  245.8 112.3 reduce-scatter.1
where the time goes:
time: 384 us
  waiting for transfers between devices  257 us (67%)
  matrix products  64.6 us (17%)
  local copies, waits for them, and re-layouts  17 us (4%)
  blocking collectives  13.8 us (4%)
  between operations  13.2 us (3%)
  other arithmetic  9.37 us (2%)
  starting transfers between devices  8.97 us (2%)
    reduce_scatter x1, waiting for transfers between devices, body(): lax.psum_scatter(jnp.dot(rows, down_weight[0], preferred_element_type=jnp...  112 us
    all_gather x1, waiting for transfers between devices, body(): piece = lax.all_gather(arrived, 'seq', axis=0, tiled=True)  68 us
    all_gather x1, waiting for transfers between devices, body(): piece = lax.all_gather(keys_values, 'seq', axis=1, tiled=True)  48.3 us
    dot_general x1, matrix products, body(): jnp.dot(rows, down_weight[0], preferred_element_type=jnp.float32)  23.8 us
    all_to_all x1, waiting for transfers between devices, sent_and_summed(): lax.all_to_all(in_blocks(shard, dim, devices), axis, 0, 0, tiled=True)  18.1 us
    all_to_all x1, blocking collectives, body(): lax.all_to_all(outgoing, 'exp', split_axis=0, concat_axis=0, tiled=True)  13.8 us
    dot_general x1, matrix products, body(): jnp.einsum('kgsn,nkd->kgsd', expo.astype(jnp.bfloat16), value_rows, prefe...  13.1 us
    dot_general x1, matrix products, body(): gate = jnp.dot(piece, gate_weight[0], preferred_element_type=jnp.float32)  11.7 us
  transfers between devices with their start and end apart: 5, of which 5 were waited for; matrix products, arithmetic and copies ran while one was open for 1% of the time, Pallas kernels for 0%

commit v1 on v0

--- a/solution.py
+++ b/solution.py
@@ -41,7 +41,9 @@
     my_span = seq_index // span_devs
     scale = 1.0 / HD**0.5
     query_heads = queries.reshape(seq_rows, kv_here, group, HD)
-    piece = lax.all_gather(keys_values, "seq", axis=1, tiled=True)
+    piece = jnp.concatenate(
+        lax.all_to_all(jnp.stack([keys_values] * lax.axis_size("seq")), "seq", 0, 0), axis=1
+    )
     peak = jnp.full((kv_here, group, seq_rows), -1e30, jnp.float32)
     count = piece.shape[1]
     key_position = jnp.arange(count, dtype=jnp.int32)

time: 384 us -> 409 us (1.065)
  local copies, waits for them, and re-layouts: 17 us -> 32.7 us
  starting transfers between devices: 8.97 us -> 17.7 us
    all_to_all x0 -> x1, waiting for transfers between devices: none -> 50.9 us  [body(): lax.all_to_all(jnp.stack([keys_values] * lax.axis_size('seq')), 'seq', 0, 0)]
    all_gather x1 -> x0, waiting for transfers between devices: 48.3 us -> none  [body(): piece = lax.all_gather(keys_values, 'seq', axis=1, tiled=True)]
    another operation x0 -> x3, local copies, waits for them, and re-layouts: none -> 11.3 us  [the longest x1 4.15 us: body(): key_rows = piece[0].reshape(count, kv_here, HD)]
    all_to_all x0 -> x1, starting transfers between devices: none -> 8.53 us  [body(): lax.all_to_all(jnp.stack([keys_values] * lax.axis_size('seq')), 'seq', 0, 0)]
    slice x0 -> x2, local copies, waits for them, and re-layouts: none -> 6.72 us  [body(): value_rows = piece[1].reshape(count, kv_here, HD)]
where the time goes in v1:
time: 409 us; the launch traced here: 408 us
  waiting for transfers between devices  258 us (63%)
  matrix products  64.6 us (16%)
  local copies, waits for them, and re-layouts  32.7 us (8%)
  starting transfers between devices  17.7 us (4%)
  between operations  13.5 us (3%)
  blocking collectives  11.9 us (3%)
  other arithmetic  9.55 us (2%)
    reduce_scatter x1, waiting for transfers between devices, body(): lax.psum_scatter(jnp.dot(rows, down_weight[0], preferred_element_type=jnp...  113 us
    all_gather x1, waiting for transfers between devices, body(): piece = lax.all_gather(arrived, 'seq', axis=0, tiled=True)  70.4 us
    all_to_all x1, waiting for transfers between devices, body(): lax.all_to_all(jnp.stack([keys_values] * lax.axis_size('seq')), 'seq', 0, 0)  50.9 us
    dot_general x1, matrix products, body(): jnp.dot(rows, down_weight[0], preferred_element_type=jnp.float32)  23.8 us
    all_to_all x1, waiting for transfers between devices, sent_and_summed(): lax.all_to_all(in_blocks(shard, dim, devices), axis, 0, 0, tiled=True)  14.8 us
    dot_general x1, matrix products, body(): jnp.einsum('kgsn,nkd->kgsd', expo.astype(jnp.bfloat16), value_rows, prefe...  13.1 us
    all_to_all x1, blocking collectives, body(): lax.all_to_all(outgoing, 'exp', split_axis=0, concat_axis=0, tiled=True)  11.9 us
    dot_general x1, matrix products, body(): gate = jnp.dot(piece, gate_weight[0], preferred_element_type=jnp.float32)  11.7 us
  transfers between devices with their start and end apart: 5, of which 5 were waited for; matrix products, arithmetic and copies ran while one was open for 1% of the time, Pallas kernels for 0%

profile of v1, /device:TPU:0, one launch (start us, length us, event | category | flops | bytes accessed | tf_op | source)
XLA Modules:
  0.0 408.2 jit_solution(10059108673750025196)
XLA Ops:
  6.5 1.2 copy.19
  7.7 3.0 stack.2
  10.7 8.5 %all-to-all-start = ((bf16[32,2,128,256]{2,3,1,0:T(8,128)(2,1)}), bf16[32,2,128,256]{2,3,1,0:T(8,128)(2,1)}, u32[]{:S(2)}, u32[]{:S(2)}) async-start(bf16[32,2,128,256]{2,3,1,0:T(8,128)(2,1)} %stack.2), calls=%async_computation | async-start | bytes 8388608 | tf_op jit(solution)/shard_map/all_to_all | solution.py:45
  19.3 0.9 copy.21
  20.2 2.1 fusion.17
  22.3 50.9 %all-to-all-done = bf16[32,2,128,256]{2,3,1,0:T(8,128)(2,1)} async-done(((bf16[32,2,128,256]{2,3,1,0:T(8,128)(2,1)}), bf16[32,2,128,256]{2,3,1,0:T(8,128)(2,1)}, u32[]{:S(2)}, u32[]{:S(2)}) %all-to-all-start) | async-done | bytes 4194336 | tf_op jit(solution)/shard_map/all_to_all | solution.py:45
  73.2 4.0 fusion.56
  77.2 2.7 copy.24
  79.9 4.1 %reshape.79 = bf16[4096,2,128,1]{0,2,1,3:T(8,128)(2,1)} reshape(bf16[1,32,128,256]{2,1,3,0:T(8,128)(2,1)} %copy.24) | data formatting | bytes 4194304 | tf_op jit(solution)/shard_map/reshape;squeeze | solution.py:53
  84.1 4.3 %copy.20 = bf16[1,32,128,256]{2,1,3,0:T(8,128)(2,1)} copy(bf16[1,32,128,256]{2,3,0,1:T(8,128)(2,1)} %get-tuple-element.8) | data formatting | bytes 4194304 | tf_op jit(solution)/shard_map/slice | solution.py:52
  88.3 4.1 %reshape_squeeze.6 = bf16[4096,2,128]{0,2,1:T(8,128)(2,1)} reshape(bf16[1,32,128,256]{2,1,3,0:T(8,128)(2,1)} %copy.20) | data formatting | bytes 4194304 | tf_op jit(solution)/shard_map/reshape;squeeze | solution.py:52
  92.5 5.0 %fusion = (f32[2,5,128]{2,1,0:T(8,128)S(1)}, f32[2,4096,128,5]{2,1,3,0:T(8,128)S(1)}) fusion(pred[128,4096]{0,1:T(8,128)(4,1)S(1)} %fusion.17, bf16[128,2,5,128]{0,3,2,1:T(8,128)(2,1)} %bitcast.80, bf16[4096,2,128]{0,2,1:T(8,128)(2,1)} %reshape_squeeze.6), kind=kOutput, calls=%fused_computation.3 | convolution fusion | flops 1357904640 | bytes 23925760 | tf_op jit(solution)/shard_map/skgd,nkd->kgsn/dot_general | solution.py:55
  97.5 5.3 %fusion.1 = f32[2,5,128]{2,1,0:T(8,128)S(1)} fusion(f32[2,4096,128,5]{2,1,3,0:T(8,128)S(1)} %get-tuple-element.10, f32[2,5,128]{2,1,0:T(8,128)S(1)} %broadcast_maximum_fusion, pred[128,4096]{0,1:T(8,128)(4,1)S(1)} %fusion.17), kind=kLoop, calls=%fused_computation.4 | loop fusion | flops 26213120 | bytes 21506048 | tf_op jit(solution)/shard_map/reduce_sum | solution.py:61
  102.8 1.7 copy-done.1
  104.5 13.1 %fusion.28 = bf16[128,2,5,128]{0,3,2,1:T(8,128)(2,1)S(1)} fusion(f32[2,4096,128,5]{2,1,3,0:T(8,128)} %copy-done.1, f32[2,5,128]{2,1,0:T(8,128)S(1)} %broadcast_maximum_fusion, pred[128,4096]{0,1:T(8,128)(4,1)S(1)} %fusion.17, bf16[4096,2,128,1]{0,2,1,3:T(8,128)(2,1)} %reshape.79, f32[128,2,5]{0,2,1:T(8,128)S(1)} %bitcast.82), kind=kOutput, calls=%fused_computation.26 | convolution fusion | flops 1368719360 | bytes 23930880 | tf_op jit(solution)/shard_map/kgsn,nkd->kgsd/dot_general | solution.py:62
  117.6 7.7 %convolution_convert_fusion.1 = bf16[128,5120]{1,0:T(8,128)(2,1)} fusion(bf16[128,1280]{0,1:T(8,128)(2,1)S(1)} %bitcast.81, bf16[1280,5120]{1,0:T(8,128)(2,1)} %param.16), kind=kOutput, calls=%fused_computation.8 | convolution fusion | flops 1678376960 | bytes 14745600 | tf_op jit(solution)/shard_map/dot_general | solution.py:74
  125.3 4.6 %all-to-all-start.1 = ((bf16[4,32,5120]{2,1,0:T(8,128)(2,1)}), bf16[4,32,5120]{2,1,0:T(8,128)(2,1)}, u32[]{:S(2)}, u32[]{:S(2)}) async-start(bf16[4,32,5120]{2,1,0:T(8,128)(2,1)} %bitcast.79), calls=%async_computation.1 | async-start | bytes 2621440 | tf_op jit(solution)/shard_map/all_to_all | solution.py:18
  130.2 14.8 %all-to-all-done.1 = bf16[4,32,5120]{2,1,0:T(8,128)(2,1)} async-done(((bf16[4,32,5120]{2,1,0:T(8,128)(2,1)}), bf16[4,32,5120]{2,1,0:T(8,128)(2,1)}, u32[]{:S(2)}, u32[]{:S(2)}) %all-to-all-start.1) | async-done | bytes 1310752 | tf_op jit(solution)/shard_map/all_to_all | solution.py:18
  145.1 1.6 convert_reduce_fusion
  147.6 1.1 convolution_convert_fusion.2
  148.7 1.1 reshape.74
  149.9 11.9 %all_to_all.20 = bf16[4,12,5120]{2,1,0:T(8,128)(2,1)} all-to-all(bf16[4,12,5120]{2,1,0:T(8,128)(2,1)S(1)} %reshape.74), channel_id=1, replica_groups=mesh['seq'=32,'exp'=4] {'exp'}, dimensions={0} | all-to-all | bytes 983040 | tf_op jit(solution)/shard_map/all_to_all | solution.py:98
  161.8 2.0 reshape.75
  164.0 70.4 %all-gather.2.cloned.1.call-done = bf16[1536,5120]{1,0:T(8,128)(2,1)} async-done(((bf16[48,5120]{1,0:T(8,128)(2,1)}), bf16[1536,5120]{1,0:T(8,128)(2,1)}) %all-gather.2.cloned.1.call-update) | async-done | bytes 15728656 | tf_op jit(solution)/shard_map/all_gather | solution.py:101
  234.4 11.7 %fusion.9 = f32[1536,256]{1,0:T(8,128)} fusion(bf16[1536,5120]{1,0:T(8,128)(2,1)} %all-gather.2.cloned.1.call-done, bf16[1,5120,256]{2,1,0:T(8,128)(2,1)} %param.17), kind=kOutput, calls=%fused_computation.15 | convolution fusion | flops 4026531840 | bytes 19922944 | tf_op jit(solution)/shard_map/dot_general | solution.py:102
  246.1 23.8 %convolution_convert_fusion = bf16[1536,5120]{1,0:T(8,128)(2,1)} fusion(bf16[1,256,5120]{2,1,0:T(8,128)(2,1)S(1)} %copy-done, bf16[1536,5120]{1,0:T(8,128)(2,1)} %all-gather.2.cloned.1.call-done, bf16[1,5120,256]{2,1,0:T(8,128)(2,1)} %param.18, f32[1536,256]{1,0:T(8,128)} %fusion.9), kind=kOutput, calls=%fused_computation.2 | convolution fusion | flops 8063287296 | bytes 38273024 | tf_op jit(solution)/shard_map/dot_general | solution.py:107
  269.9 112.5 %reduce-scatter.2.cloned.1.call-done = bf16[48,5120]{1,0:T(8,128)(2,1)} async-done(((bf16[1536,5120]{1,0:T(8,128)(2,1)}), bf16[48,5120]{1,0:T(8,128)(2,1)}) %reduce-scatter.2.cloned.1.call-update) | async-done | bytes 491536 | tf_op jit(solution)/shard_map/reduce_scatter | solution.py:106
  382.4 2.0 reshape.76
  384.4 4.3 %all-to-all-start.3 = ((bf16[4,12,5120]{2,1,0:T(8,128)(2,1)}), bf16[4,12,5120]{2,1,0:T(8,128)(2,1)S(1)}, u32[]{:S(2)}, u32[]{:S(2)}) async-start(bf16[4,12,5120]{2,1,0:T(8,128)(2,1)} %reshape.76), calls=%async_computation.4 | async-start | bytes 1310720 | tf_op jit(solution)/shard_map/all_to_all | solution.py:112
  388.7 9.6 %all-to-all-done.3 = bf16[4,12,5120]{2,1,0:T(8,128)(2,1)S(1)} async-done(((bf16[4,12,5120]{2,1,0:T(8,128)(2,1)}), bf16[4,12,5120]{2,1,0:T(8,128)(2,1)S(1)}, u32[]{:S(2)}, u32[]{:S(2)}) %all-to-all-start.3) | async-done | bytes 491552 | tf_op jit(solution)/shard_map/all_to_all | solution.py:112
  398.3 0.9 reshape.77
  399.2 2.1 fusion.6
  (29 shorter events, 1.6 us)
Async XLA Ops:
  6.5 239.6 %copy-start = (bf16[1,256,5120]{2,1,0:T(8,128)(2,1)S(1)}, bf16[1,256,5120]{2,1,0:T(8,128)(2,1)}, u32[]{:S(2)}) copy-start(bf16[1,256,5120]{2,1,0:T(8,128)(2,1)} %param.19) | copy-start | bytes 7864324
  10.7 8.6 %copy-start.3 = (bf16[128,1280]{1,0:T(8,128)(2,1)S(1)}, bf16[128,1280]{1,0:T(8,128)(2,1)}, u32[]{:S(2)}) copy-start(bf16[128,1280]{1,0:T(8,128)(2,1)} %param.10) | copy-start | bytes 983044
  10.7 62.5 %all-to-all-start = ((bf16[32,2,128,256]{2,3,1,0:T(8,128)(2,1)}), bf16[32,2,128,256]{2,3,1,0:T(8,128)(2,1)}, u32[]{:S(2)}, u32[]{:S(2)}) async-start(bf16[32,2,128,256]{2,3,1,0:T(8,128)(2,1)} %stack.2), calls=%async_computation | async-start | bytes 8388608 | tf_op jit(solution)/shard_map/all_to_all | solution.py:45
  97.5 7.0 %copy-start.1 = (f32[2,4096,128,5]{2,1,3,0:T(8,128)}, f32[2,4096,128,5]{2,1,3,0:T(8,128)S(1)}, u32[]{:S(2)}) copy-start(f32[2,4096,128,5]{2,1,3,0:T(8,128)S(1)} %get-tuple-element.10) | copy-start | bytes 62914564
  117.6 12.4 %copy-start.5 = (s32[32,1]{0,1:T(1,128)S(1)}, s32[32,1]{0,1:T(1,128)}, u32[]{:S(2)}) copy-start(s32[32,1]{0,1:T(1,128)} %param.15) | copy-start | bytes 388
  125.3 21.3 %copy-start.4 = (bf16[32,5120]{1,0:T(8,128)(2,1)S(1)}, bf16[32,5120]{1,0:T(8,128)(2,1)}, u32[]{:S(2)}) copy-start(bf16[32,5120]{1,0:T(8,128)(2,1)} %param.12) | copy-start | bytes 983044
  125.3 21.6 %copy-start.6 = (f32[32]{0:T(128)S(1)}, f32[32]{0:T(128)}, u32[]{:S(2)}) copy-start(f32[32]{0:T(128)} %param.14) | copy-start | bytes 388
  125.3 22.3 %copy-start.7 = (f32[5120]{0:T(1024)S(1)}, f32[5120]{0:T(1024)}, u32[]{:S(2)}) copy-start(f32[5120]{0:T(1024)} %param.13) | copy-start | bytes 61444
  125.3 19.7 %all-to-all-start.1 = ((bf16[4,32,5120]{2,1,0:T(8,128)(2,1)}), bf16[4,32,5120]{2,1,0:T(8,128)(2,1)}, u32[]{:S(2)}, u32[]{:S(2)}) async-start(bf16[4,32,5120]{2,1,0:T(8,128)(2,1)} %bitcast.79), calls=%async_computation.1 | async-start | bytes 2621440 | tf_op jit(solution)/shard_map/all_to_all | solution.py:18
  129.9 104.5 %all-gather.2.cloned.1.call-start = ((), (), s32[]{:S(2)}) async-start(), calls=%async_computation.5 | async-start | bytes 16220160 | tf_op jit(solution)/shard_map/all_gather | solution.py:101
  146.9 0.7 copy-start.2
  163.8 218.7 %reduce-scatter.2.cloned.1.call-start = ((), (), s32[]{:S(2)}) async-start(), calls=%async_computation.6 | async-start | bytes 16220160 | tf_op jit(solution)/shard_map/reduce_scatter | solution.py:106
  384.4 13.9 %all-to-all-start.3 = ((bf16[4,12,5120]{2,1,0:T(8,128)(2,1)}), bf16[4,12,5120]{2,1,0:T(8,128)(2,1)S(1)}, u32[]{:S(2)}, u32[]{:S(2)}) async-start(bf16[4,12,5120]{2,1,0:T(8,128)(2,1)} %reshape.76), calls=%async_computation.4 | async-start | bytes 1310720 | tf_op jit(solution)/shard_map/all_to_all | solution.py:112
Sparse Core Ops, SparseCore 0:
  163.9 70.4 all-gather.1
  270.1 112.3 reduce-scatter.1
